TPU v7x, 256 devices: a whole 4x4x8 slice. The times are simulated.
256 devices in a mesh: depth: 8 (over y, core), lat: 32 (over x, z).
Axes of the slice: x: 4, y: 4, z: 8, core: 2. Of those that a mesh axis runs over, the one named last changes fastest.
Arguments:
- volume: float32 [256, 512, 128], P('depth', 'lat'), may hold values from -6 to 6
Outputs:
- diffused: float32 [256, 512, 128], P('depth', 'lat')
All inputs are finite; a program needn't handle non-finite values.
Results may differ from a plain program's by a relative error of at most 0.0003.
Values sent between devices are 32-bit elements; how exact they have to be, the bound alone decides.
No kernel may reach another device: no remote copies, remote signals or barrier semaphores. Data moves between devices by JAX's collectives and lax.ppermute only.
A program may use at most 64 MiB of HBM per device.

v0:
```python
import jax
import jax.numpy as jnp
from jax import lax
from jax.sharding import PartitionSpec as P

TAU = 300.0
LAMBDA = 0.5


def with_halo(block, sides, width):
    for axis, dim in sides:
        count = lax.axis_size(axis)
        forward = [(i, i + 1) for i in range(count - 1)]
        backward = [(target, source) for source, target in forward]
        low = lax.ppermute(
            lax.slice_in_dim(block, block.shape[dim] - width, None, axis=dim), axis, forward
        )
        high = lax.ppermute(lax.slice_in_dim(block, 0, width, axis=dim), axis, backward)
        block = jnp.concatenate([low, block, high], axis=dim)
    return block


def conductance(diff):
    ratio = diff / LAMBDA
    return 1.0 / (1.0 + ratio * ratio)


def shifted(field, shift_by, axis, fill):
    length = field.shape[axis]
    widths = [(0, 0)] * field.ndim
    if shift_by > 0:
        widths[axis] = (shift_by, 0)
        padded = jnp.pad(field, widths, constant_values=fill)
        return lax.slice_in_dim(padded, 0, length, axis=axis)
    widths[axis] = (0, -shift_by)
    padded = jnp.pad(field, widths, constant_values=fill)
    return lax.slice_in_dim(padded, -shift_by, length - shift_by, axis=axis)


def smooth_padded(field, axis):
    return 0.25 * (shifted(field, 1, axis, 0.0) + 2.0 * field + shifted(field, -1, axis, 0.0))


def smooth_valid(field, axis):
    length = field.shape[axis]
    before = lax.slice_in_dim(field, 0, length - 2, axis=axis)
    middle = lax.slice_in_dim(field, 1, length - 1, axis=axis)
    after = lax.slice_in_dim(field, 2, length, axis=axis)
    return 0.25 * (before + 2.0 * middle + after)


def edge_mask(count, index, total, axis):
    edges = index * count + jnp.arange(count + 1, dtype=jnp.int32) - 1
    valid = jnp.logical_and(edges >= 0, edges <= count * total - 2).astype(jnp.float32)
    shape = [1, 1, 1]
    shape[axis] = count + 1
    return valid.reshape(shape)


def cyclic_solve(lower, diag, upper, sources, axis):
    length = diag.shape[axis]
    offset = 1
    while offset < length:
        low_prev = shifted(lower, offset, axis, 0.0)
        diag_prev = shifted(diag, offset, axis, 1.0)
        up_prev = shifted(upper, offset, axis, 0.0)
        low_next = shifted(lower, -offset, axis, 0.0)
        diag_next = shifted(diag, -offset, axis, 1.0)
        up_next = shifted(upper, -offset, axis, 0.0)
        left_factor = -lower / diag_prev
        right_factor = -upper / diag_next
        sources = tuple(
            (
                source
                + left_factor * shifted(source, offset, axis, 0.0)
                + right_factor * shifted(source, -offset, axis, 0.0)
                for source in sources
            )
        )
        diag = diag + left_factor * up_prev + right_factor * low_next
        lower = left_factor * low_prev
        upper = right_factor * up_next
        offset = offset * 2
    return tuple((source / diag for source in sources))


def line_coefficients(forward, axis):
    lower = -3.0 * TAU * shifted(forward, 1, axis, 0.0)
    upper = -3.0 * TAU * forward
    return (lower, 1.0 - lower - upper, upper)


def local_spike(edges, field, axis):
    count = field.shape[axis]
    inner_lower = -3.0 * TAU * lax.slice_in_dim(edges, 0, count, axis=axis)
    inner_upper = -3.0 * TAU * lax.slice_in_dim(edges, 1, count + 1, axis=axis)
    diag = 1.0 - inner_lower - inner_upper
    shape = [1, 1, 1]
    shape[axis] = count
    position = jnp.arange(count, dtype=jnp.int32).reshape(shape)
    is_first = position == 0
    is_last = position == count - 1
    lower = jnp.where(is_first, 0.0, inner_lower)
    upper = jnp.where(is_last, 0.0, inner_upper)
    left_source = jnp.where(is_first, inner_lower, 0.0)
    right_source = jnp.where(is_last, inner_upper, 0.0)
    particular, left_spike, right_spike = cyclic_solve(
        lower, diag, upper, (field, left_source, right_source), axis
    )
    ends = []
    for solved in (particular, left_spike, right_spike):
        ends.append(lax.index_in_dim(solved, 0, axis, keepdims=False))
        ends.append(lax.index_in_dim(solved, count - 1, axis, keepdims=False))
    return (particular, left_spike, right_spike, jnp.stack(ends, axis=0)[None])


def reduced_solve(gathered):

    def sweep_down(carry, block):
        chain_prev, carry_last = carry
        first_val = block[0]
        last_val = block[1]
        left_first = block[2]
        left_last = block[3]
        right_first = block[4]
        right_last = block[5]
        pivot = 1.0 - left_first * chain_prev
        result_first = (first_val - left_first * carry_last) / pivot
        result_last = last_val - left_last * carry_last + left_last * chain_prev * result_first
        factor_first = right_first / pivot
        chain_new = right_last + left_last * chain_prev * factor_first
        return ((chain_new, result_last), (factor_first, chain_new, result_first, result_last))

    zero_lines = jnp.zeros_like(gathered[0, 0])
    _, factors = lax.scan(sweep_down, (zero_lines, zero_lines), gathered)

    def sweep_up(first_later, block):
        factor_first, chain_new, result_first, result_last = block
        first_here = result_first - factor_first * first_later
        last_here = result_last - chain_new * first_later
        return (first_here, (first_here, last_here))

    _, (firsts, lasts) = lax.scan(sweep_up, zero_lines, factors, reverse=True)
    return (firsts, lasts)


def spike_finish(particular, left_spike, right_spike, firsts, lasts, index, total, axis):
    last_prev = lax.dynamic_index_in_dim(lasts, jnp.maximum(index - 1, 0), 0, keepdims=False)
    first_next = lax.dynamic_index_in_dim(
        firsts, jnp.minimum(index + 1, total - 1), 0, keepdims=False
    )
    return (
        particular
        - left_spike * jnp.expand_dims(last_prev, axis)
        - right_spike * jnp.expand_dims(first_next, axis)
    )


def shards(volume):
    depth_total = lax.axis_size("depth")
    depth_index = lax.axis_index("depth")
    lat_total = lax.axis_size("lat")
    lat_index = lax.axis_index("lat")
    planes, rows, columns = volume.shape
    padded = with_halo(volume, (("depth", 0), ("lat", 1)), 2)
    smoothed = smooth_padded(padded, 2)
    smoothed = smooth_valid(smoothed, 1)
    smoothed = smooth_valid(smoothed, 0)
    core = smoothed[1:-1, 1:-1]
    cond_x = jnp.pad(conductance(core[:, :, 1:] - core[:, :, :-1]), ((0, 0), (0, 0), (0, 1)))
    band_y = smoothed[1:-1]
    cond_y = conductance(band_y[:, 1:] - band_y[:, :-1]) * edge_mask(rows, lat_index, lat_total, 1)
    band_z = smoothed[:, 1:-1]
    cond_z = conductance(band_z[1:] - band_z[:-1]) * edge_mask(planes, depth_index, depth_total, 0)
    lower_x, diag_x, upper_x = line_coefficients(cond_x, 2)
    (solved_x,) = cyclic_solve(lower_x, diag_x, upper_x, (volume,), 2)
    field = lax.all_to_all(volume, "lat", split_axis=2, concat_axis=1, tiled=True)
    forward = lax.all_to_all(cond_y[:, 1:], "lat", split_axis=2, concat_axis=1, tiled=True)
    count, length, width = field.shape
    flat_field = jnp.transpose(field, (1, 0, 2)).reshape(length, count * width)
    flat_forward = jnp.transpose(forward, (1, 0, 2)).reshape(length, count * width)
    lower, diag, upper = line_coefficients(flat_forward, 0)
    (solved,) = cyclic_solve(lower, diag, upper, (flat_field,), 0)
    returned = jnp.transpose(solved.reshape(length, count, width), (1, 0, 2))
    solved_y = lax.all_to_all(returned, "lat", split_axis=1, concat_axis=2, tiled=True)
    part_z, left_z, right_z, ends_z = local_spike(cond_z, volume, 0)
    gathered_z = lax.all_gather(ends_z, "depth", axis=0, tiled=True)
    firsts_z, lasts_z = reduced_solve(gathered_z)
    solved_z = spike_finish(part_z, left_z, right_z, firsts_z, lasts_z, depth_index, depth_total, 0)
    return (solved_x + solved_y + solved_z) / 3.0


def solution(mesh):
    placed = (P("depth", "lat", None),)
    return jax.shard_map(
        shards, mesh=mesh, in_specs=placed, out_specs=P("depth", "lat", None), check_vma=False
    )
```

profile of v0, /device:TPU:32, one launch (start us, length us, event | category | flops | bytes accessed | tf_op | source)
XLA Modules:
  0.0 110.6 jit_solution(14266920727948924884)
XLA Ops:
  0.0 0.7 fusion.377
  0.7 1.3 %collective-permute-start.1 = (f32[2,16,128]{2,1,0:T(8,128)S(1)}, f32[2,16,128]{2,1,0:T(8,128)S(1)}, u32[]{:S(2)}, u32[]{:S(2)}) collective-permute-start(f32[2,16,128]{2,1,0:T(8,128)S(1)} %get-tuple-element.424), channel_id=1, source_target_pairs={{32,0},{64,32},{96,64},{128,96},{160,128},{192,160},{224,192},{33,... | collective-permute-start | bytes 49160 | tf_op jit(solution)/shard_map/ppermute | solution.py:18
  2.0 3.0 %collective-permute-start = (f32[2,16,128]{2,1,0:T(8,128)S(1)}, f32[2,16,128]{2,1,0:T(8,128)S(1)}, u32[]{:S(2)}, u32[]{:S(2)}) collective-permute-start(f32[2,16,128]{2,1,0:T(8,128)S(1)} %get-tuple-element.423), channel_id=1, source_target_pairs={{0,32},{32,64},{64,96},{96,128},{128,160},{160,192},{192,224},{1,3... | collective-permute-start | bytes 49160 | tf_op jit(solution)/shard_map/ppermute | solution.py:15
  5.1 1.5 %copy.156 = f32[32,16,128]{0,1,2:T(8,128)S(1)} copy(f32[32,16,128]{2,1,0:T(8,128)} %param.5) | data formatting | bytes 524288 | tf_op args[0]
  6.5 1.2 %reshape.56 = f32[32,1,2048]{2,1,0:T(1,128)} reshape(f32[128,16,32]{2,1,0:T(8,128)S(1)} %bitcast.134) | data formatting | bytes 524288
  7.7 11.3 %all-to-all-start = ((f32[32,1,2048]{2,1,0:T(1,128)}), f32[32,1,2048]{2,1,0:T(1,128)S(1)}, u32[]{:S(2)}, u32[]{:S(2)}) async-start(f32[32,1,2048]{2,1,0:T(1,128)} %reshape.56), calls=%async_computation | async-start | bytes 524288 | tf_op jit(solution)/shard_map/all_to_all | solution.py:177
  19.2 3.4 %collective-permute-start.2 = (f32[36,2,128]{2,0,1:T(8,128)S(1)}, f32[36,2,128]{2,0,1:T(8,128)S(1)}, u32[]{:S(2)}, u32[]{:S(2)}) collective-permute-start(f32[36,2,128]{2,0,1:T(8,128)S(1)} %copy.177), channel_id=1, source_target_pairs={{0,1},{1,2},{2,3},{3,4},{4,5},{5,6},{6,7},{7,8},{8,9},{9,10},{10,1... | collective-permute-start | bytes 110600 | tf_op jit(solution)/shard_map/ppermute | solution.py:15
  22.8 2.5 %collective-permute-start.3 = (f32[36,2,128]{2,0,1:T(8,128)S(1)}, f32[36,2,128]{2,0,1:T(8,128)S(1)}, u32[]{:S(2)}, u32[]{:S(2)}) collective-permute-start(f32[36,2,128]{2,0,1:T(8,128)S(1)} %copy.178), channel_id=1, source_target_pairs={{1,0},{2,1},{3,2},{4,3},{5,4},{6,5},{7,6},{8,7},{9,8},{10,9},{11,1... | collective-permute-start | bytes 110600 | tf_op jit(solution)/shard_map/ppermute | solution.py:18
  25.3 1.8 %collective-permute-done.2 = f32[36,2,128]{2,0,1:T(8,128)S(1)} collective-permute-done((f32[36,2,128]{2,0,1:T(8,128)S(1)}, f32[36,2,128]{2,0,1:T(8,128)S(1)}, u32[]{:S(2)}, u32[]{:S(2)}) %collective-permute-start.2) | collective-permute-done | bytes 36896 | tf_op jit(solution)/shard_map/ppermute | solution.py:15
  27.2 1.8 %collective-permute-done.3 = f32[36,2,128]{2,0,1:T(8,128)S(1)} collective-permute-done((f32[36,2,128]{2,0,1:T(8,128)S(1)}, f32[36,2,128]{2,0,1:T(8,128)S(1)}, u32[]{:S(2)}, u32[]{:S(2)}) %collective-permute-start.3) | collective-permute-done | bytes 36896 | tf_op jit(solution)/shard_map/ppermute | solution.py:18
  29.8 0.5 copy.159
  30.3 1.2 %reshape.58 = f32[32,1,2048]{2,1,0:T(1,128)} reshape(f32[128,16,32]{2,1,0:T(8,128)S(1)} %bitcast.132) | data formatting | bytes 524288
  31.8 0.3 fusion.167
  32.1 0.3 fusion.120
  34.5 13.4 %all-gather = f32[48,16,128]{2,1,0:T(8,128)S(1)} all-gather(f32[6,16,128]{2,1,0:T(8,128)S(1)} %constant_dynamic-update-slice_fusion.3), channel_id=2, replica_groups=mesh['depth'=8,'lat'=32] {'depth'}, dimensions={0}, use_global_device_ids=true | all-gather | bytes 442368 | tf_op jit(solution)/shard_map/all_gather | solution.py:187
  47.9 0.4 while.40
  48.4 0.3 while.41
  48.7 0.7 fusion.239
  49.5 0.7 fusion.244
  50.2 0.3 fusion.251
  50.5 0.6 fusion.256
  51.1 0.3 fusion.263
  51.5 0.6 fusion.268
  52.1 0.3 fusion.275
  52.5 0.7 copy-done.6
  53.2 10.0 %all-to-all-start.1 = ((f32[32,1,2048]{2,1,0:T(1,128)}), f32[32,1,2048]{2,1,0:T(1,128)}, u32[]{:S(2)}, u32[]{:S(2)}) async-start(f32[32,1,2048]{2,1,0:T(1,128)} %reshape.58), calls=%async_computation.1 | async-start | bytes 524288 | tf_op jit(solution)/shard_map/all_to_all | solution.py:178
  63.2 1.3 %fusion.280 = (f32[32,16,128]{2,0,1:T(8,128)}, f32[32,16,128]{2,0,1:T(8,128)S(1)}, f32[32,16,128]{2,0,1:T(8,128)S(1)}) fusion(f32[32,16,128]{2,0,1:T(8,128)S(1)} %get-tuple-element.323, f32[32,16,128]{2,0,1:T(8,128)S(1)} %fusion.275, f32[32,16,128]{2,0,1:T(8,128)S(1)} %get-tuple-element.324, f32[32,16,128]{2,0,1:T(8,128)S(1)} %fusion.263, ...), kind=kLoop, calls=%fused_computation.488 | loop fusion | flops 917504 | bytes 2097152 | tf_op jit(solution)/shard_map/add | solution.py:74
  64.5 0.3 fusion.287
  64.8 0.5 broadcast.603
  65.4 1.2 %reduce.1 = f32[32,2048]{1,0:T(8,128)S(1)} reduce(f32[32,1,2048]{2,1,0:T(1,128)S(1)} %copy-done.7, f32[]{:T(128)} %broadcast.603), dimensions={1}, to_apply=%all_to_all.39.reduce_sub_computation | reduce | bytes 524292 | tf_op jit(solution)/shard_map/all_to_all | solution.py:177
  66.6 0.3 reshape.57
  67.0 0.3 copy.158
  67.4 0.8 reshape.52
  68.2 7.8 %all-to-all-done.1 = f32[32,1,2048]{2,1,0:T(1,128)} async-done(((f32[32,1,2048]{2,1,0:T(1,128)}), f32[32,1,2048]{2,1,0:T(1,128)}, u32[]{:S(2)}, u32[]{:S(2)}) %all-to-all-start.1) | async-done | bytes 262176 | tf_op jit(solution)/shard_map/all_to_all | solution.py:178
  76.0 2.1 %reduce = f32[32,2048]{1,0:T(8,128)S(1)} reduce(f32[32,1,2048]{2,1,0:T(1,128)} %all-to-all-done.1, f32[]{:T(128)} %broadcast.603), dimensions={1}, to_apply=%all_to_all.43.reduce_sub_computation | reduce | bytes 524292 | tf_op jit(solution)/shard_map/all_to_all | solution.py:178
  78.1 0.3 reshape.59
  78.6 0.3 copy.161
  79.2 0.7 copy-done.5
  80.0 0.8 fusion.30
  80.7 0.7 fusion.35
  81.4 0.3 fusion.42
  81.8 0.6 fusion.47
  82.4 0.3 fusion.54
  82.8 0.6 fusion.59
  83.4 0.3 fusion.66
  83.7 0.6 fusion.71
  84.4 0.3 fusion.78
  84.7 0.6 fusion.83
  85.3 0.3 fusion.90
  85.7 0.6 fusion.95
  86.3 0.3 fusion.102
  86.7 0.4 fusion.107
  87.4 0.4 copy.162
  87.8 1.4 %reshape.60 = f32[32,1,2048]{2,1,0:T(1,128)} reshape(f32[512,4,32]{2,1,0:T(4,128)S(1)} %bitcast.133) | data formatting | bytes 524288
  89.2 4.9 %all-to-all-start.2 = ((f32[32,1,2048]{2,1,0:T(1,128)}), f32[32,1,2048]{2,1,0:T(1,128)S(1)}, u32[]{:S(2)}, u32[]{:S(2)}) async-start(f32[32,1,2048]{2,1,0:T(1,128)} %reshape.60), calls=%async_computation.2 | async-start | bytes 524288 | tf_op jit(solution)/shard_map/all_to_all | solution.py:185
  94.1 1.3 %fusion.292 = (f32[32,16,128]{2,0,1:T(8,128)}, f32[32,16,128]{2,0,1:T(8,128)S(1)}, f32[32,16,128]{2,0,1:T(8,128)S(1)}) fusion(f32[32,16,128]{2,0,1:T(8,128)S(1)} %copy-done.9, f32[32,16,128]{2,0,1:T(8,128)S(1)} %fusion.287, f32[32,16,128]{2,0,1:T(8,128)S(1)} %get-tuple-element.321, f32[32,16,128]{2,0,1:T(8,128)S(1)} %fusion.275, ...), kind=kLoop, calls=%fused_computation.500 | loop fusion | flops 917504 | bytes 2097152 | tf_op jit(solution)/shard_map/add | solution.py:74
  95.4 0.6 fusion.308
  96.1 10.1 %all-to-all-done.2 = f32[32,1,2048]{2,1,0:T(1,128)S(1)} async-done(((f32[32,1,2048]{2,1,0:T(1,128)}), f32[32,1,2048]{2,1,0:T(1,128)S(1)}, u32[]{:S(2)}, u32[]{:S(2)}) %all-to-all-start.2) | async-done | bytes 262176 | tf_op jit(solution)/shard_map/all_to_all | solution.py:185
  106.2 1.2 %reduce.2 = f32[32,2048]{1,0:T(8,128)S(1)} reduce(f32[32,1,2048]{2,1,0:T(1,128)S(1)} %all-to-all-done.2, f32[]{:T(128)} %broadcast.603), dimensions={1}, to_apply=%all_to_all.47.reduce_sub_computation | reduce | bytes 524292 | tf_op jit(solution)/shard_map/all_to_all | solution.py:185
  107.4 0.5 reshape.61
  108.2 0.4 copy.165
  108.6 0.5 copy-done.2
  109.2 0.5 fusion.324
  109.7 0.9 copy.175
  (95 shorter events, 5.1 us)
Async XLA Ops:
  0.7 18.3 %collective-permute-start.1 = (f32[2,16,128]{2,1,0:T(8,128)S(1)}, f32[2,16,128]{2,1,0:T(8,128)S(1)}, u32[]{:S(2)}, u32[]{:S(2)}) collective-permute-start(f32[2,16,128]{2,1,0:T(8,128)S(1)} %get-tuple-element.424), channel_id=1, source_target_pairs={{32,0},{64,32},{96,64},{128,96},{160,128},{192,160},{224,192},{33,... | collective-permute-start | bytes 49160 | tf_op jit(solution)/shard_map/ppermute | solution.py:18
  2.0 17.1 %collective-permute-start = (f32[2,16,128]{2,1,0:T(8,128)S(1)}, f32[2,16,128]{2,1,0:T(8,128)S(1)}, u32[]{:S(2)}, u32[]{:S(2)}) collective-permute-start(f32[2,16,128]{2,1,0:T(8,128)S(1)} %get-tuple-element.423), channel_id=1, source_target_pairs={{0,32},{32,64},{64,96},{96,128},{128,160},{160,192},{192,224},{1,3... | collective-permute-start | bytes 49160 | tf_op jit(solution)/shard_map/ppermute | solution.py:15
  7.7 11.4 %copy-start = (f32[32,16,128]{2,1,0:T(8,128)S(1)}, f32[32,16,128]{2,1,0:T(8,128)}, u32[]{:S(2)}) copy-start(f32[32,16,128]{2,1,0:T(8,128)} %param.5) | copy-start | bytes 786436
  7.7 44.8 %all-to-all-start = ((f32[32,1,2048]{2,1,0:T(1,128)}), f32[32,1,2048]{2,1,0:T(1,128)S(1)}, u32[]{:S(2)}, u32[]{:S(2)}) async-start(f32[32,1,2048]{2,1,0:T(1,128)} %reshape.56), calls=%async_computation | async-start | bytes 524288 | tf_op jit(solution)/shard_map/all_to_all | solution.py:177
  19.2 7.9 %collective-permute-start.2 = (f32[36,2,128]{2,0,1:T(8,128)S(1)}, f32[36,2,128]{2,0,1:T(8,128)S(1)}, u32[]{:S(2)}, u32[]{:S(2)}) collective-permute-start(f32[36,2,128]{2,0,1:T(8,128)S(1)} %copy.177), channel_id=1, source_target_pairs={{0,1},{1,2},{2,3},{3,4},{4,5},{5,6},{6,7},{7,8},{8,9},{9,10},{10,1... | collective-permute-start | bytes 110600 | tf_op jit(solution)/shard_map/ppermute | solution.py:15
  22.8 6.2 %collective-permute-start.3 = (f32[36,2,128]{2,0,1:T(8,128)S(1)}, f32[36,2,128]{2,0,1:T(8,128)S(1)}, u32[]{:S(2)}, u32[]{:S(2)}) collective-permute-start(f32[36,2,128]{2,0,1:T(8,128)S(1)} %copy.178), channel_id=1, source_target_pairs={{1,0},{2,1},{3,2},{4,3},{5,4},{6,5},{7,6},{8,7},{9,8},{10,9},{11,1... | collective-permute-start | bytes 110600 | tf_op jit(solution)/shard_map/ppermute | solution.py:18
  34.4 13.5 %copy-start.1 = (f32[32,16,128]{2,0,1:T(8,128)}, f32[32,16,128]{2,0,1:T(8,128)S(1)}, u32[]{:S(2)}) copy-start(f32[32,16,128]{2,0,1:T(8,128)S(1)} %get-tuple-element.380) | copy-start | bytes 786436
  34.4 13.5 %copy-start.3 = (f32[32,16,128]{2,0,1:T(8,128)}, f32[32,16,128]{2,0,1:T(8,128)S(1)}, u32[]{:S(2)}) copy-start(f32[32,16,128]{2,0,1:T(8,128)S(1)} %get-tuple-element.381) | copy-start | bytes 786436
  52.5 0.7 copy-start.6
  53.2 22.8 %all-to-all-start.1 = ((f32[32,1,2048]{2,1,0:T(1,128)}), f32[32,1,2048]{2,1,0:T(1,128)}, u32[]{:S(2)}, u32[]{:S(2)}) async-start(f32[32,1,2048]{2,1,0:T(1,128)} %reshape.58), calls=%async_computation.1 | async-start | bytes 524288 | tf_op jit(solution)/shard_map/all_to_all | solution.py:178
  64.5 0.9 copy-start.7
  79.0 1.0 copy-start.5
  89.2 4.9 %copy-start.9 = (f32[32,16,128]{2,0,1:T(8,128)S(1)}, f32[32,16,128]{2,0,1:T(8,128)}, u32[]{:S(2)}) copy-start(f32[32,16,128]{2,0,1:T(8,128)} %get-tuple-element.320) | copy-start | bytes 786436
  89.2 17.0 %all-to-all-start.2 = ((f32[32,1,2048]{2,1,0:T(1,128)}), f32[32,1,2048]{2,1,0:T(1,128)S(1)}, u32[]{:S(2)}, u32[]{:S(2)}) async-start(f32[32,1,2048]{2,1,0:T(1,128)} %reshape.60), calls=%async_computation.2 | async-start | bytes 524288 | tf_op jit(solution)/shard_map/all_to_all | solution.py:185
  108.1 1.0 copy-start.2
  108.1 1.0 copy-start.4
  108.1 1.1 copy-start.8
where the time goes:
time: 111 us
  starting transfers between devices  36.4 us (33%)
  other arithmetic  23.5 us (21%)
  waiting for transfers between devices  21.6 us (19%)
  local copies, waits for them, and re-layouts  14.5 us (13%)
  blocking collectives  13.4 us (12%)
    all_gather x1, blocking collectives, shards(): gathered_z = lax.all_gather(ends_z, 'depth', axis=0, tiled=True)  13.4 us
    all_to_all x1, starting transfers between devices, shards(): lax.all_to_all(volume, 'lat', split_axis=2, concat_axis=1, tiled=True)  11.3 us
    add x20, other arithmetic, cyclic_solve(): source + left_factor * shifted(source, offset, axis, 0.0)  10.9 us
    all_to_all x1, waiting for transfers between devices, shards(): lax.all_to_all(returned, 'lat', split_axis=1, concat_axis=2, tiled=True)  10.1 us
    all_to_all x1, starting transfers between devices, shards(): lax.all_to_all(cond_y[:, 1:], 'lat', split_axis=2, concat_axis=1, tiled=T...  9.98 us
    unnamed x37, local copies, waits for them, and re-layouts  8.81 us
    all_to_all x1, waiting for transfers between devices, shards(): lax.all_to_all(cond_y[:, 1:], 'lat', split_axis=2, concat_axis=1, tiled=T...  7.83 us
    ppermute x2, starting transfers between devices, with_halo(): lax.ppermute(lax.slice_in_dim(block, block.shape[dim] - width, None, axis...  6.4 us
  transfers between devices with their start and end apart: 7, of which 4 were waited for; matrix products, arithmetic and copies ran while one was open for 17% of the time, Pallas kernels for 0%

commit v1 on v0

--- a/solution.py
+++ b/solution.py
@@ -5,6 +5,24 @@
 
 TAU = 300.0
 LAMBDA = 0.5
+
+
+def collect(value, axis, dim):
+    ways, here, step = (lax.axis_size(axis), lax.axis_index(axis), value.shape[dim])
+    lengths = [n * ways if d == dim else n for d, n in enumerate(value.shape)]
+    full = lax.dynamic_update_slice_in_dim(
+        jnp.zeros(lengths, value.dtype), value, here * step, axis=dim
+    )
+    going_up = going_down = value
+    for far in range(1, ways // 2 + 1):
+        going_up = lax.ppermute(going_up, axis, [(d, (d + 1) % ways) for d in range(ways)])
+        full = lax.dynamic_update_slice_in_dim(full, going_up, (here - far) % ways * step, axis=dim)
+        if 2 * far < ways:
+            going_down = lax.ppermute(going_down, axis, [(d, (d - 1) % ways) for d in range(ways)])
+            full = lax.dynamic_update_slice_in_dim(
+                full, going_down, (here + far) % ways * step, axis=dim
+            )
+    return full
 
 
 def with_halo(block, sides, width):
@@ -184,7 +202,7 @@
     returned = jnp.transpose(solved.reshape(length, count, width), (1, 0, 2))
     solved_y = lax.all_to_all(returned, "lat", split_axis=1, concat_axis=2, tiled=True)
     part_z, left_z, right_z, ends_z = local_spike(cond_z, volume, 0)
-    gathered_z = lax.all_gather(ends_z, "depth", axis=0, tiled=True)
+    gathered_z = collect(ends_z, "depth", 0)
     firsts_z, lasts_z = reduced_solve(gathered_z)
     solved_z = spike_finish(part_z, left_z, right_z, firsts_z, lasts_z, depth_index, depth_total, 0)
     return (solved_x + solved_y + solved_z) / 3.0

time: 111 us -> 113 us (1.018); the launches traced: 111 us -> 111 us
  blocking collectives: 13.4 us -> 0 us
  starting transfers between devices: 36.4 us -> 44.6 us
  other arithmetic: 23.5 us -> 28.4 us
  waiting for transfers between devices: 21.6 us -> 24.8 us
  local copies, waits for them, and re-layouts: 14.5 us -> 12.5 us
    all_gather x1 -> x0, blocking collectives: 13.4 us -> none  [shards(): gathered_z = lax.all_gather(ends_z, 'depth', axis=0, tiled=True)]
    ppermute x0 -> x7, starting transfers between devices: none -> 8.88 us  [the longest x3 8.85 us: collect(): lax.ppermute(going_down, axis, [(d, (d - 1) % ways) for d in range(ways)])]
    ppermute x0 -> x7, waiting for transfers between devices: none -> 8.19 us  [the longest x4 8.18 us: collect(): lax.ppermute(going_up, axis, [(d, (d + 1) % ways) for d in range(ways)])]
    dynamic_update_slice x16, other arithmetic: 0.36 us -> 6.03 us  [reduced_solve(): _, factors = lax.scan(sweep_down, (zero_lines, zero_lines), gathered)]
    all_to_all x1, waiting for transfers between devices: 10.1 us -> 5.12 us  [shards(): lax.all_to_all(returned, 'lat', split_axis=1, concat_axis=2, tiled=True)]
    unnamed x37 -> x31, local copies, waits for them, and re-layouts: 8.81 us -> 7.32 us
  transfers between devices with their start and end apart: 7 -> 14, of which waited for: 4 -> 7; matrix products, arithmetic and copies ran while one was open for 17% -> 22% of each run, Pallas kernels for 0% -> 0%
where the time goes in v1:
time: 113 us; the launch traced here: 111 us
  starting transfers between devices  44.6 us (39%)
  other arithmetic  28.4 us (25%)
  waiting for transfers between devices  24.8 us (22%)
  local copies, waits for them, and re-layouts  12.5 us (11%)
    all_to_all x1, starting transfers between devices, shards(): lax.all_to_all(volume, 'lat', split_axis=2, concat_axis=1, tiled=True)  11.3 us
    add x20, other arithmetic, cyclic_solve(): source + left_factor * shifted(source, offset, axis, 0.0)  10.1 us
    all_to_all x1, starting transfers between devices, shards(): lax.all_to_all(cond_y[:, 1:], 'lat', split_axis=2, concat_axis=1, tiled=T...  9.79 us
    ppermute x3, starting transfers between devices, collect(): lax.ppermute(going_down, axis, [(d, (d - 1) % ways) for d in range(ways)])  8.85 us
    ppermute x4, waiting for transfers between devices, collect(): lax.ppermute(going_up, axis, [(d, (d + 1) % ways) for d in range(ways)])  8.18 us
    all_to_all x1, waiting for transfers between devices, shards(): lax.all_to_all(cond_y[:, 1:], 'lat', split_axis=2, concat_axis=1, tiled=T...  7.82 us
    unnamed x31, local copies, waits for them, and re-layouts  7.32 us
    ppermute x2, starting transfers between devices, with_halo(): lax.ppermute(lax.slice_in_dim(block, block.shape[dim] - width, None, axis...  6.4 us
  transfers between devices with their start and end apart: 14, of which 7 were waited for; matrix products, arithmetic and copies ran while one was open for 22% of the time, Pallas kernels for 0%

profile of v1, /device:TPU:32, one launch (start us, length us, event | category | flops | bytes accessed | tf_op | source)
XLA Modules:
  0.0 111.5 jit_solution(12969237860602051372)
XLA Ops:
  0.0 0.7 fusion.377
  0.7 1.3 %collective-permute-start.1 = (f32[2,16,128]{2,1,0:T(8,128)S(1)}, f32[2,16,128]{2,1,0:T(8,128)S(1)}, u32[]{:S(2)}, u32[]{:S(2)}) collective-permute-start(f32[2,16,128]{2,1,0:T(8,128)S(1)} %get-tuple-element.416), channel_id=1, source_target_pairs={{32,0},{64,32},{96,64},{128,96},{160,128},{192,160},{224,192},{33,... | collective-permute-start | bytes 49160 | tf_op jit(solution)/shard_map/ppermute | solution.py:36
  2.0 3.0 %collective-permute-start = (f32[2,16,128]{2,1,0:T(8,128)S(1)}, f32[2,16,128]{2,1,0:T(8,128)S(1)}, u32[]{:S(2)}, u32[]{:S(2)}) collective-permute-start(f32[2,16,128]{2,1,0:T(8,128)S(1)} %get-tuple-element.415), channel_id=1, source_target_pairs={{0,32},{32,64},{64,96},{96,128},{128,160},{160,192},{192,224},{1,3... | collective-permute-start | bytes 49160 | tf_op jit(solution)/shard_map/ppermute | solution.py:33
  5.1 1.5 %copy.170 = f32[32,16,128]{0,1,2:T(8,128)S(1)} copy(f32[32,16,128]{2,1,0:T(8,128)} %param.5) | data formatting | bytes 524288 | tf_op args[0]
  6.5 1.2 %reshape.55 = f32[32,1,2048]{2,1,0:T(1,128)} reshape(f32[128,16,32]{2,1,0:T(8,128)S(1)} %bitcast.135) | data formatting | bytes 524288
  7.7 11.3 %all-to-all-start = ((f32[32,1,2048]{2,1,0:T(1,128)}), f32[32,1,2048]{2,1,0:T(1,128)S(1)}, u32[]{:S(2)}, u32[]{:S(2)}) async-start(f32[32,1,2048]{2,1,0:T(1,128)} %reshape.55), calls=%async_computation | async-start | bytes 524288 | tf_op jit(solution)/shard_map/all_to_all | solution.py:195
  19.2 3.4 %collective-permute-start.2 = (f32[36,2,128]{2,0,1:T(8,128)S(1)}, f32[36,2,128]{2,0,1:T(8,128)S(1)}, u32[]{:S(2)}, u32[]{:S(2)}) collective-permute-start(f32[36,2,128]{2,0,1:T(8,128)S(1)} %copy.191), channel_id=1, source_target_pairs={{0,1},{1,2},{2,3},{3,4},{4,5},{5,6},{6,7},{7,8},{8,9},{9,10},{10,1... | collective-permute-start | bytes 110600 | tf_op jit(solution)/shard_map/ppermute | solution.py:33
  22.9 2.5 %collective-permute-start.3 = (f32[36,2,128]{2,0,1:T(8,128)S(1)}, f32[36,2,128]{2,0,1:T(8,128)S(1)}, u32[]{:S(2)}, u32[]{:S(2)}) collective-permute-start(f32[36,2,128]{2,0,1:T(8,128)S(1)} %copy.192), channel_id=1, source_target_pairs={{1,0},{2,1},{3,2},{4,3},{5,4},{6,5},{7,6},{8,7},{9,8},{10,9},{11,1... | collective-permute-start | bytes 110600 | tf_op jit(solution)/shard_map/ppermute | solution.py:36
  25.4 1.7 %collective-permute-done.2 = f32[36,2,128]{2,0,1:T(8,128)S(1)} collective-permute-done((f32[36,2,128]{2,0,1:T(8,128)S(1)}, f32[36,2,128]{2,0,1:T(8,128)S(1)}, u32[]{:S(2)}, u32[]{:S(2)}) %collective-permute-start.2) | collective-permute-done | bytes 36896 | tf_op jit(solution)/shard_map/ppermute | solution.py:33
  27.2 1.9 %collective-permute-done.3 = f32[36,2,128]{2,0,1:T(8,128)S(1)} collective-permute-done((f32[36,2,128]{2,0,1:T(8,128)S(1)}, f32[36,2,128]{2,0,1:T(8,128)S(1)}, u32[]{:S(2)}, u32[]{:S(2)}) %collective-permute-start.3) | collective-permute-done | bytes 36896 | tf_op jit(solution)/shard_map/ppermute | solution.py:36
  32.7 2.9 %collective-permute-start.5 = (f32[1,6,16,128]{3,2,1,0:T(8,128)S(1)}, f32[1,6,16,128]{3,2,1,0:T(8,128)S(1)}, u32[]{:S(2)}, u32[]{:S(2)}) collective-permute-start(f32[1,6,16,128]{3,2,1,0:T(8,128)S(1)} %bitcast.145), channel_id=1, source_target_pairs={{0,224},{32,0},{64,32},{96,64},{128,96},{160,128},{192,160},{224,1... | collective-permute-start | bytes 147464 | tf_op jit(solution)/shard_map/ppermute | solution.py:21
  35.8 0.7 fusion.239
  36.6 0.7 fusion.244
  37.6 0.6 fusion.256
  38.6 0.6 fusion.268
  39.5 0.6 fusion.280
  40.5 1.3 %fusion.292 = (f32[32,16,128]{2,0,1:T(8,128)}, f32[32,16,128]{2,0,1:T(8,128)S(1)}, f32[32,16,128]{2,0,1:T(8,128)S(1)}) fusion(f32[32,16,128]{2,0,1:T(8,128)S(1)} %get-tuple-element.312, f32[32,16,128]{2,0,1:T(8,128)S(1)} %fusion.287, f32[32,16,128]{2,0,1:T(8,128)S(1)} %get-tuple-element.313, f32[32,16,128]{2,0,1:T(8,128)S(1)} %fusion.275, ...), kind=kLoop, calls=%fused_computation.500 | loop fusion | flops 917504 | bytes 2097152 | tf_op jit(solution)/shard_map/add | solution.py:92
  41.8 1.5 %fusion.308 = (f32[32,16,128]{2,0,1:T(8,128)}, f32[32,16,128]{2,0,1:T(8,128)}, f32[32,16,128]{2,0,1:T(8,128)}) fusion(f32[32,16,128]{2,0,1:T(8,128)S(1)} %get-tuple-element.310, f32[32,16,128]{2,0,1:T(8,128)S(1)} %fusion.287, f32[32,16,128]{2,0,1:T(8,128)S(1)} %get-tuple-element.311), kind=kLoop, calls=%fused_computation.516 | loop fusion | flops 786432 | bytes 1572864 | tf_op jit(solution)/shard_map/mul | solution.py:100
  43.5 0.5 copy.173
  44.0 1.2 %reshape.57 = f32[32,1,2048]{2,1,0:T(1,128)} reshape(f32[128,16,32]{2,1,0:T(8,128)S(1)} %bitcast.133) | data formatting | bytes 524288
  45.1 3.0 %collective-permute-start.7 = (f32[1,6,16,128]{3,2,1,0:T(8,128)S(1)}, f32[1,6,16,128]{3,2,1,0:T(8,128)S(1)}, u32[]{:S(2)}, u32[]{:S(2)}) collective-permute-start(f32[1,6,16,128]{3,2,1,0:T(8,128)S(1)} %collective-permute-done.5), channel_id=1, source_target_pairs={{0,224},{32,0},{64,32},{96,64},{128,96},{160,128},{192,160},{224,1... | collective-permute-start | bytes 147464 | tf_op jit(solution)/shard_map/ppermute | solution.py:21
  48.1 1.7 %collective-permute-done.6 = f32[1,6,16,128]{3,2,1,0:T(8,128)S(1)} collective-permute-done((f32[1,6,16,128]{3,2,1,0:T(8,128)S(1)}, f32[1,6,16,128]{3,2,1,0:T(8,128)S(1)}, u32[]{:S(2)}, u32[]{:S(2)}) %collective-permute-start.6) | collective-permute-done | bytes 49184 | tf_op jit(solution)/shard_map/ppermute | solution.py:18
  49.9 3.0 %collective-permute-start.9 = (f32[1,6,16,128]{3,2,1,0:T(8,128)S(1)}, f32[1,6,16,128]{3,2,1,0:T(8,128)S(1)}, u32[]{:S(2)}, u32[]{:S(2)}) collective-permute-start(f32[1,6,16,128]{3,2,1,0:T(8,128)S(1)} %collective-permute-done.7), channel_id=1, source_target_pairs={{0,224},{32,0},{64,32},{96,64},{128,96},{160,128},{192,160},{224,1... | collective-permute-start | bytes 147464 | tf_op jit(solution)/shard_map/ppermute | solution.py:21
  52.8 1.7 %collective-permute-done.8 = f32[1,6,16,128]{3,2,1,0:T(8,128)S(1)} collective-permute-done((f32[1,6,16,128]{3,2,1,0:T(8,128)S(1)}, f32[1,6,16,128]{3,2,1,0:T(8,128)S(1)}, u32[]{:S(2)}, u32[]{:S(2)}) %collective-permute-start.8) | collective-permute-done | bytes 49184 | tf_op jit(solution)/shard_map/ppermute | solution.py:18
  54.6 4.7 %collective-permute-done.10 = f32[1,6,16,128]{3,2,1,0:T(8,128)S(1)} collective-permute-done((f32[1,6,16,128]{3,2,1,0:T(8,128)S(1)}, f32[1,6,16,128]{3,2,1,0:T(8,128)S(1)}, u32[]{:S(2)}, u32[]{:S(2)}) %collective-permute-start.10) | collective-permute-done | bytes 49184 | tf_op jit(solution)/shard_map/ppermute | solution.py:18
  59.3 9.8 %all-to-all-start.1 = ((f32[32,1,2048]{2,1,0:T(1,128)}), f32[32,1,2048]{2,1,0:T(1,128)S(1)}, u32[]{:S(2)}, u32[]{:S(2)}) async-start(f32[32,1,2048]{2,1,0:T(1,128)} %reshape.57), calls=%async_computation.1 | async-start | bytes 524288 | tf_op jit(solution)/shard_map/all_to_all | solution.py:196
  69.2 0.4 while.40
  69.6 0.5 broadcast.610
  70.2 1.2 %reduce.1 = f32[32,2048]{1,0:T(8,128)S(1)} reduce(f32[32,1,2048]{2,1,0:T(1,128)S(1)} %all-to-all-done, f32[]{:T(128)} %broadcast.610), dimensions={1}, to_apply=%all_to_all.39.reduce_sub_computation | reduce | bytes 524292 | tf_op jit(solution)/shard_map/all_to_all | solution.py:195
  72.3 7.8 %all-to-all-done.1 = f32[32,1,2048]{2,1,0:T(1,128)S(1)} async-done(((f32[32,1,2048]{2,1,0:T(1,128)}), f32[32,1,2048]{2,1,0:T(1,128)S(1)}, u32[]{:S(2)}, u32[]{:S(2)}) %all-to-all-start.1) | async-done | bytes 262176 | tf_op jit(solution)/shard_map/all_to_all | solution.py:196
  80.1 1.2 %reduce = f32[32,2048]{1,0:T(8,128)S(1)} reduce(f32[32,1,2048]{2,1,0:T(1,128)S(1)} %all-to-all-done.1, f32[]{:T(128)} %broadcast.610), dimensions={1}, to_apply=%all_to_all.43.reduce_sub_computation | reduce | bytes 524292 | tf_op jit(solution)/shard_map/all_to_all | solution.py:196
  82.4 0.8 fusion.30
  83.1 0.7 fusion.35
  83.8 0.3 fusion.42
  84.2 0.6 fusion.47
  84.8 0.3 fusion.54
  85.1 0.6 fusion.59
  85.8 0.3 fusion.66
  86.1 0.6 fusion.71
  86.7 0.3 fusion.78
  87.1 0.6 fusion.83
  87.7 0.3 fusion.90
  88.0 0.6 fusion.95
  88.7 0.3 fusion.102
  89.0 0.3 fusion.107
  89.7 0.4 copy.176
  90.1 1.4 %reshape.59 = f32[32,1,2048]{2,1,0:T(1,128)} reshape(f32[512,4,32]{2,1,0:T(4,128)S(1)} %bitcast.134) | data formatting | bytes 524288
  91.5 4.5 %all-to-all-start.2 = ((f32[32,1,2048]{2,1,0:T(1,128)}), f32[32,1,2048]{2,1,0:T(1,128)S(1)}, u32[]{:S(2)}, u32[]{:S(2)}) async-start(f32[32,1,2048]{2,1,0:T(1,128)} %reshape.59), calls=%async_computation.2 | async-start | bytes 524288 | tf_op jit(solution)/shard_map/all_to_all | solution.py:203
  96.0 5.8 %while.41 = (s32[]{:T(128)}, f32[16,128]{1,0:T(8,128)S(1)}, f32[8,16,128]{2,1,0:T(8,128)S(1)}, f32[8,16,128]{2,1,0:T(8,128)S(1)}, f32[8,16,128]{2,1,0:T(8,128)},...) while((s32[]{:T(128)}, f32[16,128]{1,0:T(8,128)S(1)}, ...), condition=%wide.region_3.4_spmd.clone, body=%wide.region_2.3_spmd.clone.sunk | while | flops 10244 | bytes 65679 | solution.py:161
  96.0 0.7 bitcast_dynamic-update-slice_fusion.9
  96.8 0.7 bitcast_dynamic-update-slice_fusion.9
  97.5 0.7 bitcast_dynamic-update-slice_fusion.9
  98.2 0.7 bitcast_dynamic-update-slice_fusion.9
  98.9 0.7 bitcast_dynamic-update-slice_fusion.9
  99.7 0.7 bitcast_dynamic-update-slice_fusion.9
  100.4 0.7 bitcast_dynamic-update-slice_fusion.9
  101.1 0.7 bitcast_dynamic-update-slice_fusion.9
  101.9 5.1 %all-to-all-done.2 = f32[32,1,2048]{2,1,0:T(1,128)S(1)} async-done(((f32[32,1,2048]{2,1,0:T(1,128)}), f32[32,1,2048]{2,1,0:T(1,128)S(1)}, u32[]{:S(2)}, u32[]{:S(2)}) %all-to-all-start.2) | async-done | bytes 262176 | tf_op jit(solution)/shard_map/all_to_all | solution.py:203
  107.0 1.2 %reduce.2 = f32[32,2048]{1,0:T(8,128)S(1)} reduce(f32[32,1,2048]{2,1,0:T(1,128)S(1)} %all-to-all-done.2, f32[]{:T(128)} %broadcast.610), dimensions={1}, to_apply=%all_to_all.47.reduce_sub_computation | reduce | bytes 524292 | tf_op jit(solution)/shard_map/all_to_all | solution.py:203
  108.1 0.5 reshape.60
  108.9 0.4 copy.179
  109.4 0.5 copy-done.1
  110.1 0.5 fusion.324
  110.6 0.9 copy.189
  (111 shorter events, 8.5 us)
Async XLA Ops:
  0.7 18.3 %collective-permute-start.1 = (f32[2,16,128]{2,1,0:T(8,128)S(1)}, f32[2,16,128]{2,1,0:T(8,128)S(1)}, u32[]{:S(2)}, u32[]{:S(2)}) collective-permute-start(f32[2,16,128]{2,1,0:T(8,128)S(1)} %get-tuple-element.416), channel_id=1, source_target_pairs={{32,0},{64,32},{96,64},{128,96},{160,128},{192,160},{224,192},{33,... | collective-permute-start | bytes 49160 | tf_op jit(solution)/shard_map/ppermute | solution.py:36
  2.0 17.1 %collective-permute-start = (f32[2,16,128]{2,1,0:T(8,128)S(1)}, f32[2,16,128]{2,1,0:T(8,128)S(1)}, u32[]{:S(2)}, u32[]{:S(2)}) collective-permute-start(f32[2,16,128]{2,1,0:T(8,128)S(1)} %get-tuple-element.415), channel_id=1, source_target_pairs={{0,32},{32,64},{64,96},{96,128},{128,160},{160,192},{192,224},{1,3... | collective-permute-start | bytes 49160 | tf_op jit(solution)/shard_map/ppermute | solution.py:33
  7.7 11.4 %copy-start = (f32[32,16,128]{2,1,0:T(8,128)S(1)}, f32[32,16,128]{2,1,0:T(8,128)}, u32[]{:S(2)}) copy-start(f32[32,16,128]{2,1,0:T(8,128)} %param.5) | copy-start | bytes 786436
  7.7 51.6 %all-to-all-start = ((f32[32,1,2048]{2,1,0:T(1,128)}), f32[32,1,2048]{2,1,0:T(1,128)S(1)}, u32[]{:S(2)}, u32[]{:S(2)}) async-start(f32[32,1,2048]{2,1,0:T(1,128)} %reshape.55), calls=%async_computation | async-start | bytes 524288 | tf_op jit(solution)/shard_map/all_to_all | solution.py:195
  19.2 7.9 %collective-permute-start.2 = (f32[36,2,128]{2,0,1:T(8,128)S(1)}, f32[36,2,128]{2,0,1:T(8,128)S(1)}, u32[]{:S(2)}, u32[]{:S(2)}) collective-permute-start(f32[36,2,128]{2,0,1:T(8,128)S(1)} %copy.191), channel_id=1, source_target_pairs={{0,1},{1,2},{2,3},{3,4},{4,5},{5,6},{6,7},{7,8},{8,9},{9,10},{10,1... | collective-permute-start | bytes 110600 | tf_op jit(solution)/shard_map/ppermute | solution.py:33
  22.9 6.2 %collective-permute-start.3 = (f32[36,2,128]{2,0,1:T(8,128)S(1)}, f32[36,2,128]{2,0,1:T(8,128)S(1)}, u32[]{:S(2)}, u32[]{:S(2)}) collective-permute-start(f32[36,2,128]{2,0,1:T(8,128)S(1)} %copy.192), channel_id=1, source_target_pairs={{1,0},{2,1},{3,2},{4,3},{5,4},{6,5},{7,6},{8,7},{9,8},{10,9},{11,1... | collective-permute-start | bytes 110600 | tf_op jit(solution)/shard_map/ppermute | solution.py:36
  32.6 12.5 %collective-permute-start.4 = (f32[1,6,16,128]{3,2,1,0:T(8,128)S(1)}, f32[1,6,16,128]{3,2,1,0:T(8,128)S(1)}, u32[]{:S(2)}, u32[]{:S(2)}) collective-permute-start(f32[1,6,16,128]{3,2,1,0:T(8,128)S(1)} %bitcast.144), channel_id=1, source_target_pairs={{0,32},{32,64},{64,96},{96,128},{128,160},{160,192},{192,224},{224... | collective-permute-start | bytes 147464 | tf_op jit(solution)/shard_map/ppermute | solution.py:18
  32.7 12.5 %collective-permute-start.5 = (f32[1,6,16,128]{3,2,1,0:T(8,128)S(1)}, f32[1,6,16,128]{3,2,1,0:T(8,128)S(1)}, u32[]{:S(2)}, u32[]{:S(2)}) collective-permute-start(f32[1,6,16,128]{3,2,1,0:T(8,128)S(1)} %bitcast.145), channel_id=1, source_target_pairs={{0,224},{32,0},{64,32},{96,64},{128,96},{160,128},{192,160},{224,1... | collective-permute-start | bytes 147464 | tf_op jit(solution)/shard_map/ppermute | solution.py:21
  45.1 4.7 %collective-permute-start.6 = (f32[1,6,16,128]{3,2,1,0:T(8,128)S(1)}, f32[1,6,16,128]{3,2,1,0:T(8,128)S(1)}, u32[]{:S(2)}, u32[]{:S(2)}) collective-permute-start(f32[1,6,16,128]{3,2,1,0:T(8,128)S(1)} %collective-permute-done.4), channel_id=1, source_target_pairs={{0,32},{32,64},{64,96},{96,128},{128,160},{160,192},{192,224},{224... | collective-permute-start | bytes 147464 | tf_op jit(solution)/shard_map/ppermute | solution.py:18
  45.1 4.7 %collective-permute-start.7 = (f32[1,6,16,128]{3,2,1,0:T(8,128)S(1)}, f32[1,6,16,128]{3,2,1,0:T(8,128)S(1)}, u32[]{:S(2)}, u32[]{:S(2)}) collective-permute-start(f32[1,6,16,128]{3,2,1,0:T(8,128)S(1)} %collective-permute-done.5), channel_id=1, source_target_pairs={{0,224},{32,0},{64,32},{96,64},{128,96},{160,128},{192,160},{224,1... | collective-permute-start | bytes 147464 | tf_op jit(solution)/shard_map/ppermute | solution.py:21
  49.8 4.7 %collective-permute-start.8 = (f32[1,6,16,128]{3,2,1,0:T(8,128)S(1)}, f32[1,6,16,128]{3,2,1,0:T(8,128)S(1)}, u32[]{:S(2)}, u32[]{:S(2)}) collective-permute-start(f32[1,6,16,128]{3,2,1,0:T(8,128)S(1)} %collective-permute-done.6), channel_id=1, source_target_pairs={{0,32},{32,64},{64,96},{96,128},{128,160},{160,192},{192,224},{224... | collective-permute-start | bytes 147464 | tf_op jit(solution)/shard_map/ppermute | solution.py:18
  49.9 4.7 %collective-permute-start.9 = (f32[1,6,16,128]{3,2,1,0:T(8,128)S(1)}, f32[1,6,16,128]{3,2,1,0:T(8,128)S(1)}, u32[]{:S(2)}, u32[]{:S(2)}) collective-permute-start(f32[1,6,16,128]{3,2,1,0:T(8,128)S(1)} %collective-permute-done.7), channel_id=1, source_target_pairs={{0,224},{32,0},{64,32},{96,64},{128,96},{160,128},{192,160},{224,1... | collective-permute-start | bytes 147464 | tf_op jit(solution)/shard_map/ppermute | solution.py:21
  54.6 4.7 %collective-permute-start.10 = (f32[1,6,16,128]{3,2,1,0:T(8,128)S(1)}, f32[1,6,16,128]{3,2,1,0:T(8,128)S(1)}, u32[]{:S(2)}, u32[]{:S(2)}) collective-permute-start(f32[1,6,16,128]{3,2,1,0:T(8,128)S(1)} %collective-permute-done.8), channel_id=1, source_target_pairs={{0,32},{32,64},{64,96},{96,128},{128,160},{160,192},{192,224},{224... | collective-permute-start | bytes 147464 | tf_op jit(solution)/shard_map/ppermute | solution.py:18
  59.3 20.8 %all-to-all-start.1 = ((f32[32,1,2048]{2,1,0:T(1,128)}), f32[32,1,2048]{2,1,0:T(1,128)S(1)}, u32[]{:S(2)}, u32[]{:S(2)}) async-start(f32[32,1,2048]{2,1,0:T(1,128)} %reshape.57), calls=%async_computation.1 | async-start | bytes 524288 | tf_op jit(solution)/shard_map/all_to_all | solution.py:196
  69.6 1.7 %copy-start.5 = (f32[8,16,128]{2,1,0:T(8,128)}, f32[8,16,128]{2,1,0:T(8,128)S(1)}, u32[]{:S(2)}) copy-start(f32[8,16,128]{2,1,0:T(8,128)S(1)} %get-tuple-element.584) | copy-start | bytes 196612
  69.6 1.7 %copy-start.6 = (f32[8,16,128]{2,1,0:T(8,128)}, f32[8,16,128]{2,1,0:T(8,128)S(1)}, u32[]{:S(2)}) copy-start(f32[8,16,128]{2,1,0:T(8,128)S(1)} %get-tuple-element.586) | copy-start | bytes 196612
  91.5 15.5 %all-to-all-start.2 = ((f32[32,1,2048]{2,1,0:T(1,128)}), f32[32,1,2048]{2,1,0:T(1,128)S(1)}, u32[]{:S(2)}, u32[]{:S(2)}) async-start(f32[32,1,2048]{2,1,0:T(1,128)} %reshape.59), calls=%async_computation.2 | async-start | bytes 524288 | tf_op jit(solution)/shard_map/all_to_all | solution.py:203
  108.9 1.0 copy-start.1
  108.9 1.0 copy-start.2
  108.9 1.1 copy-start.3
  108.9 1.2 %copy-start.4 = (f32[32,16,128]{2,0,1:T(8,128)S(1)}, f32[32,16,128]{2,0,1:T(8,128)}, u32[]{:S(2)}) copy-start(f32[32,16,128]{2,0,1:T(8,128)} %get-tuple-element.309) | copy-start | bytes 786436
